TPU v7x, 128 devices: a whole 4x4x4 slice. The times are simulated.
128 devices in a mesh: queue: 32 (over y, x, z_lo), head: 4 (over z_hi, core).
Axes of the slice: x: 4, y: 4, z: 4 (z_hi: 2, z_lo: 2; z = z_hi * 2 + z_lo), core: 2. Of those that a mesh axis runs over, the one named last changes fastest.
Arguments:
- latents: bfloat16 [64, 384, 5120], P('queue'), may hold values from -6 to 6
- control: bfloat16 [64, 384, 5120], P('queue'), may hold values from -3 to 3
- levels: int32 [64], P('queue'), may hold values from 0 to 63
- window_mask: int32 [64, 2], P('queue'), may hold values 0 or 1
- modulation: float32 [64, 3, 5120], replicated, may hold values from -3 to 3
- w_query: bfloat16 [5120, 2560], P('queue', 'head'), may hold values from -1 to 1
- w_key: bfloat16 [5120, 2560], P('queue', 'head'), may hold values from -1 to 1
- w_value: bfloat16 [5120, 2560], P('queue', 'head'), may hold values from -0.078125 to 0.078125
- w_out: bfloat16 [2560, 5120], P('head', 'queue'), may hold values from -0.125 to 0.125
- q_gain: float32 [2560], P('head'), may hold values from 0.6 to 8
- k_gain: float32 [2560], P('head'), may hold values from 0.6 to 8
Outputs:
- next_queue: float32 [64, 384, 5120], P('queue', None, 'head')
All inputs are finite; a program needn't handle non-finite values. No bound on the sum of `window_mask` on one device may be relied on, other than what follows from the above.
Results may differ from a plain program's by a relative error of at most 0.019.
The roundings to bfloat16 on the way count: a program that leaves them out, or rounds other values in their place, can miss the bound.
Values may be sent and summed in bfloat16 or wider, within the bound.
A program may use at most 192 MiB of HBM per device.

v0:
```python
import jax
import jax.numpy as jnp
from jax import lax
from jax.sharding import PartitionSpec as P

HD = 128


def from_behind(value, axis, by):
    peers = lax.axis_size(axis)
    pairs = [(i, i + by) for i in range(peers) if 0 <= i + by < peers]
    return lax.ppermute(value, axis, pairs)


def shifted(value, axis, steps):
    count = lax.axis_size(axis)
    pairs = [(source, (source + steps) % count) for source in range(count)]
    return lax.ppermute(value, axis, pairs)


def layer_norm(hidden):
    center = hidden - jnp.mean(hidden, axis=-1, keepdims=True)
    variance = jnp.mean(center * center, axis=-1, keepdims=True)
    return center * lax.rsqrt(variance + 1e-06)


def apply_gain(values, square_sum, total_width, gain):
    floats = values.astype(jnp.float32)
    return (floats * lax.rsqrt(square_sum[:, None] / total_width + 1e-06) * gain).astype(
        jnp.bfloat16
    )


def row_squares(values):
    floats = values.astype(jnp.float32)
    return jnp.sum(floats * floats, axis=-1)


def shards(
    latents,
    control,
    levels,
    window_mask,
    modulation,
    w_query,
    w_key,
    w_value,
    w_out,
    q_gain,
    k_gain,
):
    nchunk, row_count, model_width = latents.shape
    level_count = modulation.shape[0]
    local_cols = w_query.shape[1]
    heads_local = local_cols // HD
    head_count = lax.axis_size("head")
    total_width = local_cols * head_count
    owner_index = lax.axis_index("queue")
    head_index = lax.axis_index("head")
    first_span = owner_index * nchunk
    hidden = latents.astype(jnp.float32) + control.astype(jnp.float32)
    onehot = (levels[:, None] == jnp.arange(level_count, dtype=jnp.int32)[None, :]).astype(
        jnp.float32
    )
    level_mods = jnp.dot(
        onehot, modulation.reshape(level_count, 3 * model_width), precision=lax.Precision.HIGHEST
    ).reshape(nchunk, 3, model_width)
    normed = (
        layer_norm(hidden) * (1.0 + level_mods[:, 1][:, None, :]) + level_mods[:, 0][:, None, :]
    ).astype(jnp.bfloat16)
    flat_rows = normed.reshape(nchunk * row_count, model_width)
    row_total = nchunk * row_count
    pieces = (
        lax.all_gather(w_query, "queue", axis=0, tiled=True),
        lax.all_gather(w_key, "queue", axis=0, tiled=True),
        lax.all_gather(w_value, "queue", axis=0, tiled=True),
    )
    query, keyproj, valueproj = tuple(
        (
            jnp.dot(flat_rows, piece_rows, preferred_element_type=jnp.float32)
            for piece_rows in pieces
        )
    )
    query = query.astype(jnp.bfloat16)
    keyproj = keyproj.astype(jnp.bfloat16)
    valueproj = valueproj.astype(jnp.bfloat16)
    query_sq, key_sq = lax.psum((row_squares(query), row_squares(keyproj)), "head")
    qhat = apply_gain(query, query_sq, total_width, q_gain)
    own_keys = apply_gain(keyproj, key_sq, total_width, k_gain)
    prior_keys, prior_values = from_behind((own_keys, valueproj), "queue", 1)
    key_stack = jnp.concatenate([prior_keys, own_keys], axis=0).reshape(
        2 * nchunk, row_count, heads_local, HD
    )
    value_stack = jnp.concatenate([prior_values, valueproj], axis=0).reshape(
        2 * nchunk, row_count, heads_local, HD
    )
    key_windows = jnp.stack(
        [
            key_stack[nchunk + index_span - 2 : nchunk + index_span + 1]
            for index_span in range(nchunk)
        ]
    ).reshape(nchunk, 3 * row_count, heads_local, HD)
    value_windows = jnp.stack(
        [
            value_stack[nchunk + index_span - 2 : nchunk + index_span + 1]
            for index_span in range(nchunk)
        ]
    ).reshape(nchunk, 3 * row_count, heads_local, HD)
    span_ids = first_span + jnp.arange(nchunk, dtype=jnp.int32)
    seen_far = (window_mask[:, 0] == 1) & (span_ids >= 2)
    seen_near = (window_mask[:, 1] == 1) & (span_ids >= 1)
    seen = jnp.stack([seen_far, seen_near, jnp.ones((nchunk,), dtype=bool)], axis=1)
    key_seen = jnp.repeat(seen, row_count, axis=1)
    query_spans = qhat.reshape(nchunk, row_count, heads_local, HD)
    scores = jnp.einsum(
        "cqhd,ckhd->chqk", query_spans, key_windows, preferred_element_type=jnp.float32
    ) * HD ** (-0.5)
    scores = jnp.where(key_seen[:, None, None, :], scores, -1e30)
    top = jnp.max(scores, axis=-1, keepdims=True)
    expo = jnp.exp(scores - top)
    prob_bf = (expo / jnp.sum(expo, axis=-1, keepdims=True)).astype(jnp.bfloat16)
    attended = jnp.einsum(
        "chqk,ckhd->cqhd", prob_bf, value_windows, preferred_element_type=jnp.float32
    )
    attended = attended.astype(jnp.bfloat16).reshape(row_total, local_cols)
    partial_out = jnp.dot(
        attended,
        lax.all_gather(w_out, "queue", axis=1, tiled=True),
        preferred_element_type=jnp.float32,
    )
    col_width = model_width // head_count
    hidden_cols = lax.dynamic_slice_in_dim(hidden, head_index * col_width, col_width, 2)
    gate_cols = lax.dynamic_slice_in_dim(level_mods[:, 2], head_index * col_width, col_width, 1)
    branch = (
        lax.psum_scatter(partial_out.astype(jnp.bfloat16), "head", scatter_dimension=1, tiled=True)
        .astype(jnp.float32)
        .reshape(nchunk, row_count, col_width)
    )
    updated = hidden_cols + gate_cols[:, None, :] * branch
    arrived = shifted(updated[nchunk - 1].astype(jnp.bfloat16), "queue", 1).astype(jnp.float32)
    return jnp.concatenate([arrived[None], updated[: nchunk - 1]], axis=0)


def solution(mesh):
    placed = (
        P("queue", None, None),
        P("queue", None, None),
        P("queue"),
        P("queue", None),
        P(),
        P("queue", "head"),
        P("queue", "head"),
        P("queue", "head"),
        P("head", "queue"),
        P("head"),
        P("head"),
    )
    return jax.shard_map(
        shards, mesh=mesh, in_specs=placed, out_specs=P("queue", None, "head"), check_vma=False
    )
```

profile of v0, /device:TPU:0, one launch (start us, length us, event | category | flops | bytes accessed | tf_op | source)
XLA Modules:
  0.0 834.2 jit_solution(3768649909468280332)
XLA Ops:
  6.5 0.7 all-gather.7.cloned.1.call-update
  7.3 0.0 all-gather.9.cloned.1.call-start
  7.3 0.7 all-gather.9.cloned.1.call-update
  8.0 0.0 all-gather.5.cloned.1.call-start
  8.1 0.7 all-gather.5.cloned.1.call-update
  8.7 0.0 all-gather.11.cloned.1.call-start
  8.8 0.5 all-gather.11.cloned.1.call-update
  9.3 0.0 reduce-scatter.2.cloned.1.call-start
  9.4 0.0 slice-start
  9.4 0.0 slice-start.1
  9.4 13.7 %convert_add_fusion = (f32[2,384,5120]{2,1,0:T(8,128)}, f32[2,384]{1,0:T(2,128)S(1)}) fusion(bf16[2,384,5120]{2,1,0:T(8,128)(2,1)} %param.12, bf16[2,384,5120]{2,1,0:T(8,128)(2,1)} %param.11), kind=kLoop, calls=%fused_computation.6 | loop fusion | flops 15727872 | bytes 31460352 | tf_op jit(solution)/shard_map/add | solution.py:61
  23.1 0.0 slice-done.1
  23.1 0.0 copy-start.4
  23.1 0.0 copy-start.5
  23.1 6.4 multiply_reduce_fusion
  29.5 0.1 compare_and_fusion.1
  29.6 0.1 pad.8.clone
  29.7 0.1 add_add_fusion
  29.8 0.0 copy-done.5
  29.8 3.5 fusion.6
  33.3 10.8 %add_convert_fusion = bf16[2,384,5120]{2,1,0:T(8,128)(2,1)} fusion(f32[2,5120]{1,0:T(2,128)S(1)} %get-tuple-element.14, f32[2,5120]{1,0:T(2,128)S(1)} %get-tuple-element.15, f32[2,384]{1,0:T(2,128)S(1)} %add_rsqrt_fusion.2, f32[2,384]{1,0:T(2,128)S(1)} %broadcast_multiply_fusion, bf16[2,384,5120]{2,1,0:T(8,128)(2,1)} %param.12, bf16[2,384,5120]{2,1,0:T(8,128)(2,1)} %param.11), kind=kLoop, calls=%fused_computation.4 | loop fusion | flops 31457280 | bytes 23681024 | tf_op jit(solution)/shard_map/convert_element_type | solution.py:70
  44.1 132.3 %all-gather.7.cloned.1.call-done = bf16[5120,640]{1,0:T(8,128)(2,1)} async-done(((bf16[160,640]{1,0:T(8,128)(2,1)}), bf16[5120,640]{1,0:T(8,128)(2,1)}) %all-gather.7.cloned.1.call-update) | async-done | bytes 6553616 | tf_op jit(solution)/shard_map/all_gather | solution.py:74
  176.4 10.4 %fusion.17 = (f32[768]{0:T(1024)S(1)}, bf16[768,640]{0,1:T(8,128)(2,1)S(1)}) fusion(bf16[768,5120]{1,0:T(8,128)(2,1)} %bitcast.59, bf16[5120,640]{1,0:T(8,128)(2,1)} %all-gather.7.cloned.1.call-done), kind=kOutput, calls=%fused_computation.30 | convolution fusion | flops 5035129856 | bytes 15404032 | tf_op jit(solution)/shard_map/dot_general | solution.py:80
  186.8 0.0 copy-start.2
  186.8 153.5 %all-gather.9.cloned.1.call-done = bf16[5120,640]{1,0:T(8,128)(2,1)} async-done(((bf16[160,640]{1,0:T(8,128)(2,1)}), bf16[5120,640]{1,0:T(8,128)(2,1)}) %all-gather.9.cloned.1.call-update) | async-done | bytes 6553616 | tf_op jit(solution)/shard_map/all_gather | solution.py:75
  340.4 10.6 %fusion.20 = (f32[768]{0:T(1024)S(1)}, bf16[768,640]{1,0:T(8,128)(2,1)S(1)}) fusion(bf16[768,5120]{1,0:T(8,128)(2,1)} %bitcast.60, bf16[5120,640]{1,0:T(8,128)(2,1)} %all-gather.9.cloned.1.call-done), kind=kOutput, calls=%fused_computation.33 | convolution fusion | flops 5035129856 | bytes 15404032 | tf_op jit(solution)/shard_map/dot_general | solution.py:80
  351.0 7.7 all-reduce
  358.7 0.3 fusion.22
  359.0 0.0 copy-start
  359.0 0.0 copy-start.3
  359.1 2.4 collective-permute-start.1
  361.4 163.7 %all-gather.5.cloned.1.call-done = bf16[5120,640]{1,0:T(8,128)(2,1)} async-done(((bf16[160,640]{1,0:T(8,128)(2,1)}), bf16[5120,640]{1,0:T(8,128)(2,1)}) %all-gather.5.cloned.1.call-update) | async-done | bytes 6553616 | tf_op jit(solution)/shard_map/all_gather | solution.py:76
  525.1 11.3 %convolution_convert_fusion.3 = bf16[768,640]{1,0:T(8,128)(2,1)} fusion(bf16[768,5120]{1,0:T(8,128)(2,1)} %bitcast.61, bf16[5120,640]{1,0:T(8,128)(2,1)} %all-gather.5.cloned.1.call-done), kind=kOutput, calls=%fused_computation.48 | convolution fusion | flops 5033656320 | bytes 15400960 | tf_op jit(solution)/shard_map/dot_general | solution.py:80
  536.4 0.0 copy-done
  536.4 2.5 collective-permute-start
  538.9 0.1 broadcast_bitcast_fusion
  539.0 0.3 fusion.19
  539.3 1.2 reshape.85
  540.5 0.0 collective-permute-done.1
  540.5 2.0 fusion.27
  542.5 2.1 copy.21
  544.6 3.6 copy.23
  548.2 0.9 copy.22
  549.1 2.1 copy.24
  551.2 12.5 %collective-permute-done = bf16[768,640]{1,0:T(8,128)(2,1)} collective-permute-done((bf16[768,640]{1,0:T(8,128)(2,1)}, bf16[768,640]{1,0:T(8,128)(2,1)}, u32[]{:S(2)}, u32[]{:S(2)}) %collective-permute-start) | collective-permute-done | bytes 983072 | tf_op jit(solution)/shard_map/ppermute | solution.py:12
  563.8 2.0 fusion.28
  565.8 2.2 copy.19
  568.0 0.9 copy.20
  569.0 0.0 copy-start.1
  569.0 14.5 %fusion.56 = (f32[2,5,384]{2,1,0:T(8,128)S(1)}, f32[2,5,384,1152]{3,2,1,0:T(8,128)}) fusion(pred[2,1152]{1,0:T(4,128)(4,1)S(1)} %bitcast.69, bf16[1,1152,5,128]{3,1,2,0:T(8,128)(2,1)} %copy.24, bf16[1,1152,5,128]{3,1,2,0:T(8,128)(2,1)} %copy.23, bf16[2,384,5,128]{1,0,3,2:T(2,128)(2,1)} %reshape.85), kind=kOutput, calls=%fused_computation.78 | convolution fusion | flops 1151632512 | bytes 21644544 | tf_op jit(solution)/shard_map/sub | solution.py:120
  583.5 7.8 fusion.32
  591.3 1.0 copy.26
  592.3 0.2 copy.30
  592.5 114.0 %all-gather.11.cloned.1.call-done = bf16[640,5120]{0,1:T(8,128)(2,1)} async-done(((bf16[640,160]{0,1:T(8,128)(2,1)}), bf16[640,5120]{0,1:T(8,128)(2,1)}) %all-gather.11.cloned.1.call-update) | async-done | bytes 6553616 | tf_op jit(solution)/shard_map/all_gather | solution.py:128
  706.4 11.4 %convolution_convert_fusion = bf16[768,5120]{1,0:T(8,128)(2,1)} fusion(bf16[768,640]{0,1:T(8,128)(2,1)S(1)} %bitcast.68, bf16[640,5120]{0,1:T(8,128)(2,1)} %all-gather.11.cloned.1.call-done), kind=kOutput, calls=%fused_computation.12 | convolution fusion | flops 5037096960 | bytes 15400960 | tf_op jit(solution)/shard_map/dot_general | solution.py:126
  717.9 0.0 reduce-scatter.2.cloned.1.call-update
  717.9 76.6 %reduce-scatter.2.cloned.1.call-done = bf16[768,1280]{1,0:T(8,128)(2,1)} async-done(((bf16[768,5120]{1,0:T(8,128)(2,1)}), bf16[768,1280]{1,0:T(8,128)(2,1)}) %reduce-scatter.2.cloned.1.call-update) | async-done | bytes 1966096 | tf_op jit(solution)/shard_map/reduce_scatter | solution.py:135
  794.6 3.1 fusion.9
  797.7 0.1 fusion.35
  797.8 0.7 collective-permute-start.2
  798.5 0.1 slice.57
  798.6 26.8 %collective-permute-done.2 = bf16[384,1280]{1,0:T(8,128)(2,1)S(1)} collective-permute-done((bf16[384,1280]{1,0:T(8,128)(2,1)S(1)}, bf16[384,1280]{1,0:T(8,128)(2,1)S(1)}, u32[]{:S(2)}, u32[]{:S(2)}) %collective-permute-start.2) | collective-permute-done | bytes 983072 | tf_op jit(solution)/shard_map/ppermute | solution.py:18
  825.4 0.1 bitcast_convert_fusion
  825.5 2.2 pad_maximum_fusion
  (14 shorter events, 0.1 us)
Async XLA Ops:
  6.5 169.8 %all-gather.7.cloned.1.call-start = ((), (), s32[]{:S(2)}) async-start(), calls=%async_computation.2 | async-start | bytes 6758400 | tf_op jit(solution)/shard_map/all_gather | solution.py:74
  7.3 333.1 %all-gather.9.cloned.1.call-start = ((), (), s32[]{:S(2)}) async-start(), calls=%async_computation.3 | async-start | bytes 6758400 | tf_op jit(solution)/shard_map/all_gather | solution.py:75
  8.0 517.1 %all-gather.5.cloned.1.call-start = ((), (), s32[]{:S(2)}) async-start(), calls=%async_computation.1 | async-start | bytes 6758400 | tf_op jit(solution)/shard_map/all_gather | solution.py:76
  8.7 697.7 %all-gather.11.cloned.1.call-start = ((), (), s32[]{:S(2)}) async-start(), calls=%async_computation.4 | async-start | bytes 6758400 | tf_op jit(solution)/shard_map/all_gather | solution.py:128
  9.3 785.2 %reduce-scatter.2.cloned.1.call-start = ((), (), s32[]{:S(2)}) async-start(), calls=%async_computation.5 | async-start | bytes 9830400 | tf_op jit(solution)/shard_map/reduce_scatter | solution.py:135
  9.4 13.7 %slice-start = ((s8[7864320]{0:T(1024)(128)(4,1)}), s8[4194304]{0:T(1024)(128)(4,1)S(1)}, s32[]{:S(2)}) async-start(s8[7864320]{0:T(1024)(128)(4,1)} %bitcast.57), calls=%async_computation.6 | async-start | bytes 8388608
  9.4 13.7 %slice-start.1 = ((s8[7864320]{0:T(1024)(128)(4,1)}), s8[3670016]{0:T(1024)(128)(4,1)S(1)}, s32[]{:S(2)}) async-start(s8[7864320]{0:T(1024)(128)(4,1)} %bitcast.57), calls=%async_computation.7 | async-start | bytes 7340032
  23.1 6.4 copy-start.4
  23.1 6.7 copy-start.5
  186.8 171.9 %copy-start.2 = (f32[640]{0:T(1024)S(1)}, f32[640]{0:T(1024)}, u32[]{:S(2)}) copy-start(f32[640]{0:T(1024)} %param.21) | copy-start | bytes 7684
  359.0 177.3 %copy-start = (bf16[768,640]{1,0:T(8,128)(2,1)}, bf16[768,640]{1,0:T(8,128)(2,1)S(1)}, u32[]{:S(2)}) copy-start(bf16[768,640]{1,0:T(8,128)(2,1)S(1)} %fusion.22) | copy-start | bytes 2949124
  359.0 179.9 %copy-start.3 = (f32[640]{0:T(1024)S(1)}, f32[640]{0:T(1024)}, u32[]{:S(2)}) copy-start(f32[640]{0:T(1024)} %param.20) | copy-start | bytes 7684
  359.1 181.4 %collective-permute-start.1 = (bf16[768,640]{1,0:T(8,128)(2,1)S(1)}, bf16[768,640]{1,0:T(8,128)(2,1)}, u32[]{:S(2)}, u32[]{:S(2)}) collective-permute-start(bf16[768,640]{1,0:T(8,128)(2,1)S(1)} %fusion.22), channel_id=1, source_target_pairs={{0,4},{4,8},{8,12},{12,16},{16,20},{20,24},{24,28},{28,32},{32,36}... | collective-permute-start | bytes 2949128 | tf_op jit(solution)/shard_map/ppermute | solution.py:12
  536.4 27.4 %collective-permute-start = (bf16[768,640]{1,0:T(8,128)(2,1)}, bf16[768,640]{1,0:T(8,128)(2,1)}, u32[]{:S(2)}, u32[]{:S(2)}) collective-permute-start(bf16[768,640]{1,0:T(8,128)(2,1)} %convolution_convert_fusion.3), channel_id=1, source_target_pairs={{0,4},{4,8},{8,12},{12,16},{16,20},{20,24},{24,28},{28,32},{32,36}... | collective-permute-start | bytes 2949128 | tf_op jit(solution)/shard_map/ppermute | solution.py:12
  569.0 14.5 %copy-start.1 = (bf16[1152,640]{0,1:T(8,128)(2,1)S(1)}, bf16[1152,640]{0,1:T(8,128)(2,1)}, u32[]{:S(2)}) copy-start(bf16[1152,640]{0,1:T(8,128)(2,1)} %copy.19) | copy-start | bytes 4423684
  797.8 27.6 %collective-permute-start.2 = (bf16[384,1280]{1,0:T(8,128)(2,1)S(1)}, bf16[384,1280]{1,0:T(8,128)(2,1)S(1)}, u32[]{:S(2)}, u32[]{:S(2)}) collective-permute-start(bf16[384,1280]{1,0:T(8,128)(2,1)S(1)} %fusion.35), channel_id=1, source_target_pairs={{0,4},{4,8},{8,12},{12,16},{16,20},{20,24},{24,28},{28,32},{32,36}... | collective-permute-start | bytes 2949128 | tf_op jit(solution)/shard_map/ppermute | solution.py:18
Sparse Core Ops, SparseCore 0:
  9.0 167.3 all-gather.6
  178.0 162.3 all-gather.8
  342.0 183.0 all-gather.4
  526.6 179.8 all-gather.10
  718.0 76.5 reduce-scatter.1
where the time goes:
time: 835 us; the launch traced here: 834 us
  waiting for transfers between devices  682 us (82%)
  matrix products  69.5 us (8%)
  other arithmetic  41.2 us (5%)
  local copies, waits for them, and re-layouts  14.7 us (2%)
  between operations  13.4 us (2%)
    all_gather x1, waiting for transfers between devices, shards(): lax.all_gather(w_value, 'queue', axis=0, tiled=True)  164 us
    all_gather x1, waiting for transfers between devices, shards(): lax.all_gather(w_key, 'queue', axis=0, tiled=True)  154 us
    all_gather x1, waiting for transfers between devices, shards(): lax.all_gather(w_query, 'queue', axis=0, tiled=True)  132 us
    all_gather x1, waiting for transfers between devices, shards(): lax.all_gather(w_out, 'queue', axis=1, tiled=True)  114 us
    reduce_scatter x1, waiting for transfers between devices, shards(): lax.psum_scatter(partial_out.astype(jnp.bfloat16), 'head', scatter_dimens...  76.6 us
    dot_general x3, matrix products, shards(): jnp.dot(flat_rows, piece_rows, preferred_element_type=jnp.float32)  32.4 us
    ppermute x1, waiting for transfers between devices, shifted(): return lax.ppermute(value, axis, pairs)  26.8 us
  transfers between devices with their start and end apart: 8, of which 7 were waited for; matrix products, arithmetic and copies ran while one was open for 13% of the time, Pallas kernels for 0%

commit v1 on v0

--- a/solution.py
+++ b/solution.py
@@ -4,6 +4,11 @@
 from jax.sharding import PartitionSpec as P
 
 HD = 128
+
+
+def all_by_exchange(array, name, dim):
+    sent = jnp.stack([array] * lax.axis_size(name))
+    return jnp.concatenate(lax.all_to_all(sent, name, 0, 0), axis=dim)
 
 
 def from_behind(value, axis, by):
@@ -71,7 +76,7 @@
     flat_rows = normed.reshape(nchunk * row_count, model_width)
     row_total = nchunk * row_count
     pieces = (
-        lax.all_gather(w_query, "queue", axis=0, tiled=True),
+        all_by_exchange(w_query, "queue", 0),
         lax.all_gather(w_key, "queue", axis=0, tiled=True),
         lax.all_gather(w_value, "queue", axis=0, tiled=True),
     )

time: 835 us -> 773 us (0.926)
  waiting for transfers between devices: 682 us -> 600 us
  starting transfers between devices: 5.76 us -> 16.8 us
    all_gather x1 -> x0, waiting for transfers between devices: 132 us -> none  [shards(): lax.all_gather(w_query, 'queue', axis=0, tiled=True)]
    all_to_all x0 -> x1, waiting for transfers between devices: none -> 79.9 us  [all_by_exchange(): return jnp.concatenate(lax.all_to_all(sent, name, 0, 0), axis=dim)]
    all_gather x1, waiting for transfers between devices: 154 us -> 121 us  [shards(): lax.all_gather(w_key, 'queue', axis=0, tiled=True)]
    all_to_all x0 -> x1, starting transfers between devices: none -> 9.03 us  [all_by_exchange(): return jnp.concatenate(lax.all_to_all(sent, name, 0, 0), axis=dim)]
  transfers between devices with their start and end apart: 8 -> 8, of which waited for: 7 -> 7; matrix products, arithmetic and copies ran while one was open for 13% -> 15% of each run, Pallas kernels for 0% -> 0%
where the time goes in v1:
time: 773 us; the launch traced here: 767 us
  waiting for transfers between devices  600 us (78%)
  matrix products  69.8 us (9%)
  other arithmetic  39.8 us (5%)
  local copies, waits for them, and re-layouts  18.8 us (2%)
  starting transfers between devices  16.8 us (2%)
  between operations  13.6 us (2%)
  blocking collectives  7.96 us (1%)
    all_gather x1, waiting for transfers between devices, shards(): lax.all_gather(w_value, 'queue', axis=0, tiled=True)  162 us
    all_gather x1, waiting for transfers between devices, shards(): lax.all_gather(w_key, 'queue', axis=0, tiled=True)  121 us
    all_gather x1, waiting for transfers between devices, shards(): lax.all_gather(w_out, 'queue', axis=1, tiled=True)  113 us
    reduce_scatter x1, waiting for transfers between devices, shards(): lax.psum_scatter(partial_out.astype(jnp.bfloat16), 'head', scatter_dimens...  83.7 us
    all_to_all x1, waiting for transfers between devices, all_by_exchange(): return jnp.concatenate(lax.all_to_all(sent, name, 0, 0), axis=dim)  79.9 us
    dot_general x3, matrix products, shards(): jnp.dot(flat_rows, piece_rows, preferred_element_type=jnp.float32)  32.4 us
    ppermute x1, waiting for transfers between devices, shifted(): return lax.ppermute(value, axis, pairs)  26.8 us
  transfers between devices with their start and end apart: 8, of which 7 were waited for; matrix products, arithmetic and copies ran while one was open for 15% of the time, Pallas kernels for 0%

profile of v1, /device:TPU:0, one launch (start us, length us, event | category | flops | bytes accessed | tf_op | source)
XLA Modules:
  0.0 766.8 jit_solution(14859837709388380833)
XLA Ops:
  6.5 0.0 all-gather.6.cloned.1.call-start
  6.5 0.7 all-gather.6.cloned.1.call-update
  7.3 0.0 all-gather.4.cloned.1.call-start
  7.3 0.7 all-gather.4.cloned.1.call-update
  8.0 4.1 stack.20
  12.1 9.0 %all-to-all-start = ((bf16[32,160,640]{2,1,0:T(8,128)(2,1)}), bf16[32,160,640]{2,1,0:T(8,128)(2,1)}, u32[]{:S(2)}, u32[]{:S(2)}) async-start(bf16[32,160,640]{2,1,0:T(8,128)(2,1)} %stack.20), calls=%async_computation | async-start | bytes 13107200 | tf_op jit(solution)/shard_map/all_to_all | solution.py:11
  21.2 0.0 all-gather.8.cloned.1.call-start
  21.2 0.7 all-gather.8.cloned.1.call-update
  21.9 0.0 reduce-scatter.2.cloned.1.call-start
  21.9 0.1 pad.8.clone
  22.0 0.0 copy-done.4
  22.0 0.1 compare_and_fusion.1
  22.1 0.1 add_add_fusion
  22.2 13.6 %convert_add_fusion = (f32[2,384,5120]{2,1,0:T(8,128)}, f32[2,384]{1,0:T(2,128)S(1)}) fusion(bf16[2,384,5120]{2,1,0:T(8,128)(2,1)} %param.12, bf16[2,384,5120]{2,1,0:T(8,128)(2,1)} %param.11), kind=kLoop, calls=%fused_computation.6 | loop fusion | flops 15727872 | bytes 31460352 | tf_op jit(solution)/shard_map/add | solution.py:66
  35.8 0.0 slice-done
  35.8 0.0 slice-done.1
  35.8 0.0 copy-start.5
  35.8 6.4 multiply_reduce_fusion
  42.2 0.0 copy-done.5
  42.2 3.5 fusion.6
  45.7 9.6 %add_convert_fusion = bf16[2,384,5120]{2,1,0:T(8,128)(2,1)} fusion(f32[2,5120]{1,0:T(2,128)S(1)} %get-tuple-element.14, f32[2,5120]{1,0:T(2,128)S(1)} %get-tuple-element.15, f32[2,384]{1,0:T(2,128)S(1)} %add_rsqrt_fusion.2, f32[2,384]{1,0:T(2,128)S(1)} %broadcast_multiply_fusion, bf16[2,384,5120]{2,1,0:T(8,128)(2,1)S(1)} %bitcast.59, ...), kind=kLoop, calls=%fused_computation.4 | loop fusion | flops 31457280 | bytes 23681024 | tf_op jit(solution)/shard_map/convert_element_type | solution.py:75
  55.3 79.9 %all-to-all-done = bf16[32,160,640]{2,1,0:T(8,128)(2,1)} async-done(((bf16[32,160,640]{2,1,0:T(8,128)(2,1)}), bf16[32,160,640]{2,1,0:T(8,128)(2,1)}, u32[]{:S(2)}, u32[]{:S(2)}) %all-to-all-start) | async-done | bytes 6553632 | tf_op jit(solution)/shard_map/all_to_all | solution.py:11
  135.2 10.5 %fusion.17 = (f32[768]{0:T(1024)S(1)}, bf16[768,640]{0,1:T(8,128)(2,1)S(1)}) fusion(bf16[768,5120]{1,0:T(8,128)(2,1)} %bitcast.60, bf16[5120,640]{1,0:T(8,128)(2,1)} %bitcast.8), kind=kOutput, calls=%fused_computation.30 | convolution fusion | flops 5035129856 | bytes 15404032 | tf_op jit(solution)/shard_map/dot_general | solution.py:85
  145.7 0.0 copy-start.2
  145.7 120.5 %all-gather.6.cloned.1.call-done = bf16[5120,640]{1,0:T(8,128)(2,1)} async-done(((bf16[160,640]{1,0:T(8,128)(2,1)}), bf16[5120,640]{1,0:T(8,128)(2,1)}) %all-gather.6.cloned.1.call-update) | async-done | bytes 6553616 | tf_op jit(solution)/shard_map/all_gather | solution.py:80
  266.3 10.6 %fusion.20 = (f32[768]{0:T(1024)S(1)}, bf16[768,640]{1,0:T(8,128)(2,1)S(1)}) fusion(bf16[768,5120]{1,0:T(8,128)(2,1)} %bitcast.61, bf16[5120,640]{1,0:T(8,128)(2,1)} %all-gather.6.cloned.1.call-done), kind=kOutput, calls=%fused_computation.33 | convolution fusion | flops 5035129856 | bytes 15404032 | tf_op jit(solution)/shard_map/dot_general | solution.py:85
  276.9 8.0 %all-reduce = (f32[768]{0:T(1024)S(1)}, f32[768]{0:T(1024)S(1)}) all-reduce(f32[768]{0:T(1024)S(1)} %get-tuple-element.18, f32[768]{0:T(1024)S(1)} %get-tuple-element.20), channel_id=1, replica_groups=mesh['queue'=32,'head'=4] {'head'}, use_global_device_ids=true, to_apply=%region_5.0 | all-reduce | flops 1536 | bytes 12288 | tf_op jit(solution)/shard_map/psum | solution.py:92
  284.9 0.0 copy-done.2
  284.9 0.3 fusion.22
  285.2 0.0 copy-start
  285.2 0.0 copy-start.3
  285.3 3.1 collective-permute-start.1
  288.4 162.1 %all-gather.4.cloned.1.call-done = bf16[5120,640]{1,0:T(8,128)(2,1)} async-done(((bf16[160,640]{1,0:T(8,128)(2,1)}), bf16[5120,640]{1,0:T(8,128)(2,1)}) %all-gather.4.cloned.1.call-update) | async-done | bytes 6553616 | tf_op jit(solution)/shard_map/all_gather | solution.py:81
  450.5 11.3 %convolution_convert_fusion.3 = bf16[768,640]{1,0:T(8,128)(2,1)} fusion(bf16[768,5120]{1,0:T(8,128)(2,1)} %bitcast.62, bf16[5120,640]{1,0:T(8,128)(2,1)} %all-gather.4.cloned.1.call-done), kind=kOutput, calls=%fused_computation.48 | convolution fusion | flops 5033656320 | bytes 15400960 | tf_op jit(solution)/shard_map/dot_general | solution.py:85
  461.7 3.7 collective-permute-start
  465.5 0.1 broadcast_bitcast_fusion
  465.6 0.0 copy-done.3
  465.6 0.3 fusion.19
  465.9 1.2 reshape.91
  467.1 0.0 collective-permute-done.1
  467.1 2.0 fusion.27
  469.1 2.1 copy.21
  471.2 3.6 copy.23
  474.8 0.9 copy.22
  475.8 2.1 copy.24
  477.9 12.4 %collective-permute-done = bf16[768,640]{1,0:T(8,128)(2,1)} collective-permute-done((bf16[768,640]{1,0:T(8,128)(2,1)}, bf16[768,640]{1,0:T(8,128)(2,1)}, u32[]{:S(2)}, u32[]{:S(2)}) %collective-permute-start) | collective-permute-done | bytes 983072 | tf_op jit(solution)/shard_map/ppermute | solution.py:17
  490.3 2.0 fusion.28
  492.3 2.2 copy.19
  494.5 0.9 copy.20
  495.5 14.5 %fusion.56 = (f32[2,5,384]{2,1,0:T(8,128)S(1)}, f32[2,5,384,1152]{3,2,1,0:T(8,128)}) fusion(pred[2,1152]{1,0:T(4,128)(4,1)S(1)} %bitcast.70, bf16[1,1152,5,128]{3,1,2,0:T(8,128)(2,1)} %copy.24, bf16[1,1152,5,128]{3,1,2,0:T(8,128)(2,1)} %copy.23, bf16[2,384,5,128]{1,0,3,2:T(2,128)(2,1)} %reshape.91), kind=kOutput, calls=%fused_computation.78 | convolution fusion | flops 1151632512 | bytes 21644544 | tf_op jit(solution)/shard_map/sub | solution.py:125
  510.0 7.8 %fusion.32 = bf16[2,384,5,128]{1,3,2,0:T(8,128)(2,1)S(1)} fusion(f32[2,5,384,1152]{3,2,1,0:T(8,128)} %get-tuple-element.23, f32[2,5,384]{2,1,0:T(8,128)S(1)} %get-tuple-element.22, bf16[1,1152,5,128]{1,3,2,0:T(8,128)(2,1)S(1)} %bitcast.68, bf16[1,1152,5,128]{1,3,2,0:T(8,128)(2,1)S(1)} %bitcast.67), kind=kOutput, calls=%fused_computation.49 | convolution fusion | flops 1143275520 | bytes 21642240 | tf_op jit(solution)/shard_map/chqk,ckhd->cqhd/dot_general | solution.py:127
  517.8 1.0 copy.26
  518.8 0.2 copy.30
  519.0 112.6 %all-gather.8.cloned.1.call-done = bf16[640,5120]{0,1:T(8,128)(2,1)} async-done(((bf16[640,160]{0,1:T(8,128)(2,1)}), bf16[640,5120]{0,1:T(8,128)(2,1)}) %all-gather.8.cloned.1.call-update) | async-done | bytes 6553616 | tf_op jit(solution)/shard_map/all_gather | solution.py:133
  631.5 11.6 %convolution_convert_fusion = bf16[768,5120]{1,0:T(8,128)(2,1)} fusion(bf16[768,640]{0,1:T(8,128)(2,1)S(1)} %bitcast.69, bf16[640,5120]{0,1:T(8,128)(2,1)} %all-gather.8.cloned.1.call-done), kind=kOutput, calls=%fused_computation.12 | convolution fusion | flops 5037096960 | bytes 15400960 | tf_op jit(solution)/shard_map/dot_general | solution.py:131
  643.2 0.0 reduce-scatter.2.cloned.1.call-update
  643.2 83.7 %reduce-scatter.2.cloned.1.call-done = bf16[768,1280]{1,0:T(8,128)(2,1)} async-done(((bf16[768,5120]{1,0:T(8,128)(2,1)}), bf16[768,1280]{1,0:T(8,128)(2,1)}) %reduce-scatter.2.cloned.1.call-update) | async-done | bytes 1966096 | tf_op jit(solution)/shard_map/reduce_scatter | solution.py:140
  726.9 3.1 fusion.9
  730.0 0.1 fusion.35
  730.1 0.7 collective-permute-start.2
  730.8 0.1 slice.57
  730.9 26.8 %collective-permute-done.2 = bf16[384,1280]{1,0:T(8,128)(2,1)S(1)} collective-permute-done((bf16[384,1280]{1,0:T(8,128)(2,1)S(1)}, bf16[384,1280]{1,0:T(8,128)(2,1)S(1)}, u32[]{:S(2)}, u32[]{:S(2)}) %collective-permute-start.2) | collective-permute-done | bytes 983072 | tf_op jit(solution)/shard_map/ppermute | solution.py:23
  757.7 0.1 bitcast_convert_fusion
  757.8 2.2 pad_maximum_fusion
  (14 shorter events, 0.1 us)
Async XLA Ops:
  6.5 259.8 %all-gather.6.cloned.1.call-start = ((), (), s32[]{:S(2)}) async-start(), calls=%async_computation.3 | async-start | bytes 6758400 | tf_op jit(solution)/shard_map/all_gather | solution.py:80
  7.3 443.2 %all-gather.4.cloned.1.call-start = ((), (), s32[]{:S(2)}) async-start(), calls=%async_computation.2 | async-start | bytes 6758400 | tf_op jit(solution)/shard_map/all_gather | solution.py:81
  12.1 9.9 %copy-start.4 = (s32[2,2]{1,0:T(2,128)S(1)}, s32[2,2]{1,0:T(2,128)}, u32[]{:S(2)}) copy-start(s32[2,2]{1,0:T(2,128)} %param.14) | copy-start | bytes 52
  12.1 123.1 %all-to-all-start = ((bf16[32,160,640]{2,1,0:T(8,128)(2,1)}), bf16[32,160,640]{2,1,0:T(8,128)(2,1)}, u32[]{:S(2)}, u32[]{:S(2)}) async-start(bf16[32,160,640]{2,1,0:T(8,128)(2,1)} %stack.20), calls=%async_computation | async-start | bytes 13107200 | tf_op jit(solution)/shard_map/all_to_all | solution.py:11
  21.2 610.4 %all-gather.8.cloned.1.call-start = ((), (), s32[]{:S(2)}) async-start(), calls=%async_computation.4 | async-start | bytes 6758400 | tf_op jit(solution)/shard_map/all_gather | solution.py:133
  21.9 705.0 %reduce-scatter.2.cloned.1.call-start = ((), (), s32[]{:S(2)}) async-start(), calls=%async_computation.5 | async-start | bytes 9830400 | tf_op jit(solution)/shard_map/reduce_scatter | solution.py:140
  22.1 13.7 %slice-start = ((s8[7864320]{0:T(1024)(128)(4,1)}), s8[4194304]{0:T(1024)(128)(4,1)S(1)}, s32[]{:S(2)}) async-start(s8[7864320]{0:T(1024)(128)(4,1)} %bitcast.58), calls=%async_computation.6 | async-start | bytes 8388608
  22.2 13.6 %slice-start.1 = ((s8[7864320]{0:T(1024)(128)(4,1)}), s8[3670016]{0:T(1024)(128)(4,1)S(1)}, s32[]{:S(2)}) async-start(s8[7864320]{0:T(1024)(128)(4,1)} %bitcast.58), calls=%async_computation.7 | async-start | bytes 7340032
  35.8 6.4 copy-start.5
  145.7 139.2 %copy-start.2 = (f32[640]{0:T(1024)S(1)}, f32[640]{0:T(1024)}, u32[]{:S(2)}) copy-start(f32[640]{0:T(1024)} %param.21) | copy-start | bytes 7684
  285.2 176.5 %copy-start = (bf16[768,640]{1,0:T(8,128)(2,1)}, bf16[768,640]{1,0:T(8,128)(2,1)S(1)}, u32[]{:S(2)}) copy-start(bf16[768,640]{1,0:T(8,128)(2,1)S(1)} %fusion.22) | copy-start | bytes 2949124
  285.2 180.3 %copy-start.3 = (f32[640]{0:T(1024)S(1)}, f32[640]{0:T(1024)}, u32[]{:S(2)}) copy-start(f32[640]{0:T(1024)} %param.20) | copy-start | bytes 7684
  285.3 181.8 %collective-permute-start.1 = (bf16[768,640]{1,0:T(8,128)(2,1)S(1)}, bf16[768,640]{1,0:T(8,128)(2,1)}, u32[]{:S(2)}, u32[]{:S(2)}) collective-permute-start(bf16[768,640]{1,0:T(8,128)(2,1)S(1)} %fusion.22), channel_id=1, source_target_pairs={{0,4},{4,8},{8,12},{12,16},{16,20},{20,24},{24,28},{28,32},{32,36}... | collective-permute-start | bytes 2949128 | tf_op jit(solution)/shard_map/ppermute | solution.py:17
  461.7 28.6 %collective-permute-start = (bf16[768,640]{1,0:T(8,128)(2,1)}, bf16[768,640]{1,0:T(8,128)(2,1)}, u32[]{:S(2)}, u32[]{:S(2)}) collective-permute-start(bf16[768,640]{1,0:T(8,128)(2,1)} %convolution_convert_fusion.3), channel_id=1, source_target_pairs={{0,4},{4,8},{8,12},{12,16},{16,20},{20,24},{24,28},{28,32},{32,36}... | collective-permute-start | bytes 2949128 | tf_op jit(solution)/shard_map/ppermute | solution.py:17
  495.5 14.6 %copy-start.1 = (bf16[1152,640]{0,1:T(8,128)(2,1)S(1)}, bf16[1152,640]{0,1:T(8,128)(2,1)}, u32[]{:S(2)}) copy-start(bf16[1152,640]{0,1:T(8,128)(2,1)} %copy.19) | copy-start | bytes 4423684
  730.1 27.6 %collective-permute-start.2 = (bf16[384,1280]{1,0:T(8,128)(2,1)S(1)}, bf16[384,1280]{1,0:T(8,128)(2,1)S(1)}, u32[]{:S(2)}, u32[]{:S(2)}) collective-permute-start(bf16[384,1280]{1,0:T(8,128)(2,1)S(1)} %fusion.35), channel_id=1, source_target_pairs={{0,4},{4,8},{8,12},{12,16},{16,20},{20,24},{24,28},{28,32},{32,36}... | collective-permute-start | bytes 2949128 | tf_op jit(solution)/shard_map/ppermute | solution.py:23
Sparse Core Ops, SparseCore 0:
  9.0 257.2 all-gather.5
  267.9 182.4 all-gather.3
  452.1 179.3 all-gather.7
  643.3 83.5 reduce-scatter.1
